TPU v7x, 128 devices: a whole 4x4x4 slice. The times are simulated.
128 devices in a mesh: dp: 8 (over z_hi, y), tensor: 4 (over z_lo, core), replica: 4 (over x).
Axes of the slice: x: 4, y: 4, z: 4 (z_hi: 2, z_lo: 2; z = z_hi * 2 + z_lo), core: 2. Of those that a mesh axis runs over, the one named last changes fastest.
Arguments:
- queries: bfloat16 [8192, 8192], P(('dp', 'replica'), 'tensor'), may hold values from -8 to 8
- d_out: bfloat16 [8192, 8192], P(('dp', 'replica'), 'tensor'), may hold values from -48 to 48
- conv_keys: bfloat16 [8192, 1024], P(('dp', 'replica'), 'tensor'), may hold values from -12 to 12
- conv_values: bfloat16 [8192, 1024], P(('dp', 'replica'), 'tensor'), may hold values from -6 to 6
- segment_ids: int32 [32, 256], P(('dp', 'replica')), may hold values from 0 to 3, never falling along the last dimension, each value on 1 to 192 neighbouring positions
- master_keys: float32 [4096, 1024], P('dp', 'tensor'), may hold values from -8 to 8
- master_values: float32 [4096, 1024], P('dp', 'tensor'), may hold values from -6 to 6
- moment_keys: float32 [4096, 1024], P('dp', 'tensor'), may hold values from -3 to 3
- moment_values: float32 [4096, 1024], P('dp', 'tensor'), may hold values from -3 to 3
- second_keys: float32 [4096, 1024], P('dp', 'tensor'), may hold values from 0.01 to 1
- second_values: float32 [4096, 1024], P('dp', 'tensor'), may hold values from 0.01 to 1
Outputs:
- new_master_keys: float32 [4096, 1024], P('dp', 'tensor')
- new_master_values: float32 [4096, 1024], P('dp', 'tensor')
- new_moment_keys: float32 [4096, 1024], P('dp', 'tensor')
- new_moment_values: float32 [4096, 1024], P('dp', 'tensor')
- new_second_keys: float32 [4096, 1024], P('dp', 'tensor')
- new_second_values: float32 [4096, 1024], P('dp', 'tensor')
- served_keys: bfloat16 [4096, 1024], P(None, 'tensor')
- served_values: bfloat16 [4096, 1024], P(None, 'tensor')
- grad_keys: float32 [4096, 1024], P('dp', 'tensor')
- grad_values: float32 [4096, 1024], P('dp', 'tensor')
Inputs may be any that keep to these rules, and one draw needn't show every extreme that they name: `segment_ids`: each row holds the conversation numbers of one device's 256 tokens.
All inputs are finite; a program needn't handle non-finite values.
Results may differ from a plain program's by a relative error of at most 0.0065.
Values may be sent and summed in bfloat16 or wider, within the bound.
No kernel may reach another device: no remote copies, remote signals or barrier semaphores. Data moves between devices by JAX's collectives and lax.ppermute only.
A program may use at most 256 MiB of HBM per device.

v0:
```python
import jax
import jax.numpy as jnp
from jax import lax
from jax.sharding import PartitionSpec as P

Q_HEADS = 64
KV_HEADS = 8
HEAD_DIM = 128
STEP = 20
BETA_ONE = 0.9
BETA_TWO = 0.95
LEARN_RATE = 0.05
WEIGHT_DECAY = 0.1
EPSILON = 1e-08


def sent_together(arrays, axis, dim, along):
    both = jnp.concatenate(arrays, axis=along)
    filled, at, done = (lax.psum_scatter(both, axis, scatter_dimension=dim, tiled=True), 0, [])
    for a in arrays:
        done.append(lax.slice_in_dim(filled, at, at + a.shape[along], axis=along))
        at += a.shape[along]
    return tuple(done)


def from_everyone(value, axis):
    copies = jnp.broadcast_to(value, (lax.axis_size(axis), *value.shape))
    return lax.all_to_all(copies, axis, split_axis=0, concat_axis=0, tiled=True)


def of_everyone(value, axis):
    everything = from_everyone(value, axis)
    return jnp.sum(everything, axis=0)


def in_one(arrays, axis):
    ends = [0]
    for a in arrays:
        ends.append(ends[-1] + a.size)
    subtotal = of_everyone(jnp.concatenate([a.ravel() for a in arrays]), axis)
    return tuple((subtotal[b:e].reshape(a.shape) for a, b, e in zip(arrays, ends, ends[1:])))


def side_by_side(arrays, axis, dim, along):
    ends, at = ([], 0)
    for a in arrays[:-1]:
        at += a.shape[along]
        ends.append(at)
    both = jnp.concatenate(arrays, axis=along)
    return tuple(jnp.split(lax.all_gather(both, axis, axis=dim, tiled=True), ends, axis=along))


def attend_block(query_rows, grad_rows, own_keys, own_values, cart_keys, cart_values, visible):
    tokens_here, head_dim = own_keys.shape
    heads_here = query_rows.shape[1] // head_dim
    factor = head_dim ** (-0.5)
    flat_query = query_rows.reshape(tokens_here * heads_here, head_dim)
    flat_grad = grad_rows.reshape(tokens_here * heads_here, head_dim)
    cart_scores = jnp.dot(flat_query, cart_keys.T, preferred_element_type=jnp.float32) * factor
    own_scores = jnp.dot(flat_query, own_keys.T, preferred_element_type=jnp.float32) * factor
    own_scores = own_scores.reshape(tokens_here, heads_here, tokens_here)
    own_scores = jnp.where(visible[:, None, :], own_scores, -jnp.inf).reshape(
        tokens_here * heads_here, tokens_here
    )
    highest = jnp.maximum(jnp.max(cart_scores, axis=1), jnp.max(own_scores, axis=1))[:, None]
    cart_exp = jnp.exp(cart_scores - highest)
    own_exp = jnp.exp(own_scores - highest)
    denominator = jnp.sum(cart_exp, axis=1, keepdims=True) + jnp.sum(own_exp, axis=1, keepdims=True)
    cart_probs = cart_exp / denominator
    own_probs = own_exp / denominator
    cart_dprob = jnp.dot(flat_grad, cart_values.T, preferred_element_type=jnp.float32)
    own_dprob = jnp.dot(flat_grad, own_values.T, preferred_element_type=jnp.float32)
    centre = jnp.sum(cart_probs * cart_dprob, axis=1, keepdims=True) + jnp.sum(
        own_probs * own_dprob, axis=1, keepdims=True
    )
    cart_dscore = (cart_probs * (cart_dprob - centre)).astype(jnp.bfloat16)
    contract = (((0,), (0,)), ((), ()))
    grad_values = lax.dot_general(
        cart_probs.astype(jnp.bfloat16), flat_grad, contract, preferred_element_type=jnp.float32
    )
    grad_keys = (
        lax.dot_general(cart_dscore, flat_query, contract, preferred_element_type=jnp.float32)
        * factor
    )
    return (grad_keys, grad_values)


def device_grads(queries, d_out, conv_keys, conv_values, cart_keys, cart_values, segments):
    tokens_here = conv_keys.shape[0]
    head_dim = HEAD_DIM
    group_size = Q_HEADS // KV_HEADS
    half_size = group_size // 2
    kv_local = conv_keys.shape[1] // head_dim
    places = jnp.arange(tokens_here, dtype=jnp.int32)
    visible = (segments[:, None] == segments[None, :]) & (places[None, :] <= places[:, None])
    key_parts = []
    value_parts = []
    for kv_head in range(kv_local):
        col_lo = kv_head * head_dim
        col_hi = col_lo + head_dim
        key_sum = jnp.zeros((cart_keys.shape[0], head_dim), jnp.float32)
        value_sum = jnp.zeros((cart_keys.shape[0], head_dim), jnp.float32)
        for which_half in range(2):
            start_col = (kv_head * group_size + which_half * half_size) * head_dim
            end_col = start_col + half_size * head_dim
            grad_keys, grad_values = attend_block(
                queries[:, start_col:end_col],
                d_out[:, start_col:end_col],
                conv_keys[:, col_lo:col_hi],
                conv_values[:, col_lo:col_hi],
                cart_keys[:, col_lo:col_hi],
                cart_values[:, col_lo:col_hi],
                visible,
            )
            key_sum = key_sum + grad_keys
            value_sum = value_sum + grad_values
        key_parts.append(key_sum)
        value_parts.append(value_sum)
    return (jnp.concatenate(key_parts, axis=1), jnp.concatenate(value_parts, axis=1))


def adamw_step(param, moment, second, grad):
    moment_new = BETA_ONE * moment + (1.0 - BETA_ONE) * grad
    second_new = BETA_TWO * second + (1.0 - BETA_TWO) * grad * grad
    moment_hat = moment_new / (1.0 - BETA_ONE**STEP)
    second_hat = second_new / (1.0 - BETA_TWO**STEP)
    param_new = param - LEARN_RATE * (
        moment_hat / (jnp.sqrt(second_hat) + EPSILON) + WEIGHT_DECAY * param
    )
    return (param_new, moment_new, second_new)


def per_device(
    queries,
    d_out,
    conv_keys,
    conv_values,
    segment_ids,
    master_keys,
    master_values,
    moment_keys,
    moment_values,
    second_keys,
    second_values,
):
    cart_keys, cart_values = (
        lax.all_gather(master_keys.astype(jnp.bfloat16), "dp", axis=0, tiled=True),
        lax.all_gather(master_values.astype(jnp.bfloat16), "dp", axis=0, tiled=True),
    )
    grad_keys, grad_values = device_grads(
        queries, d_out, conv_keys, conv_values, cart_keys, cart_values, segment_ids[0]
    )
    key_share, value_share = sent_together((grad_keys, grad_values), "dp", 0, 1)
    shard_keys, shard_values = in_one((key_share, value_share), "replica")
    new_master_keys, new_moment_keys, new_second_keys = adamw_step(
        master_keys, moment_keys, second_keys, shard_keys
    )
    new_master_values, new_moment_values, new_second_values = adamw_step(
        master_values, moment_values, second_values, shard_values
    )
    served_keys, served_values = side_by_side(
        (new_master_keys.astype(jnp.bfloat16), new_master_values.astype(jnp.bfloat16)), "dp", 0, 1
    )
    return (
        new_master_keys,
        new_master_values,
        new_moment_keys,
        new_moment_values,
        new_second_keys,
        new_second_values,
        served_keys,
        served_values,
        shard_keys,
        shard_values,
    )


def solution(mesh):
    return jax.shard_map(
        per_device,
        mesh=mesh,
        in_specs=(
            P(("dp", "replica"), "tensor"),
            P(("dp", "replica"), "tensor"),
            P(("dp", "replica"), "tensor"),
            P(("dp", "replica"), "tensor"),
            P(("dp", "replica"), None),
            P("dp", "tensor"),
            P("dp", "tensor"),
            P("dp", "tensor"),
            P("dp", "tensor"),
            P("dp", "tensor"),
            P("dp", "tensor"),
        ),
        out_specs=(
            P("dp", "tensor"),
            P("dp", "tensor"),
            P("dp", "tensor"),
            P("dp", "tensor"),
            P("dp", "tensor"),
            P("dp", "tensor"),
            P(None, "tensor"),
            P(None, "tensor"),
            P("dp", "tensor"),
            P("dp", "tensor"),
        ),
        check_vma=False,
    )
```

profile of v0, /device:TPU:0, one launch (start us, length us, event | category | flops | bytes accessed | tf_op | source)
XLA Modules:
  0.0 544.8 jit_solution(12731431613612274478)
XLA Ops:
  7.2 1.8 convert_element_type.36
  9.1 1.8 convert_element_type.37
  11.0 0.9 fusion.64
  12.6 1.3 fusion.88
  14.7 1.4 fusion.89
  16.0 0.9 reshape.192
  16.9 0.9 reshape.194
  17.7 0.9 reshape.198
  18.6 0.9 reshape.196
  19.5 1.2 fusion.91
  20.7 1.3 fusion.90
  21.9 2.2 fusion.92
  24.2 1.3 fusion.93
  25.5 43.1 %all-gather.4.cloned.1.call-done = bf16[4096,256]{1,0:T(8,128)(2,1)} async-done(((bf16[512,256]{1,0:T(8,128)(2,1)}), bf16[4096,256]{1,0:T(8,128)(2,1)}) %all-gather.4.cloned.1.call-update) | async-done | bytes 2097168 | tf_op jit(solution)/shard_map/all_gather | solution.py:147
  68.6 9.5 %multiply_reduce_fusion.5 = (f32[1024]{0:T(1024)S(1)}, f32[1024,4096]{1,0:T(8,128)}) fusion(bf16[1024,128]{1,0:T(8,128)(2,1)} %copy-done.15, bf16[4096,256]{1,0:T(8,128)(2,1)} %all-gather.4.cloned.1.call-done), kind=kOutput, calls=%fused_computation.13 | convolution fusion | flops 1082129408 | bytes 18092032 | tf_op jit(solution)/shard_map/dot_general | solution.py:59
  78.3 8.9 %fusion.5 = f32[1024]{0:T(1024)S(1)} fusion(f32[1024,4096]{1,0:T(8,128)} %get-tuple-element.37, f32[1024]{0:T(1024)S(1)} %max.30), kind=kLoop, calls=%fused_computation.21 | loop fusion | flops 12581888 | bytes 16785408 | tf_op jit(solution)/shard_map/reduce_sum | solution.py:68
  87.2 8.1 %multiply_reduce_fusion.4 = (f32[1024]{0:T(1024)S(1)}, f32[1024,4096]{1,0:T(8,128)}) fusion(bf16[1024,128]{1,0:T(8,128)(2,1)S(1)} %reshape.197, bf16[4096,256]{1,0:T(8,128)(2,1)S(1)} %copy-done), kind=kOutput, calls=%fused_computation.12 | convolution fusion | flops 1082129408 | bytes 18092032 | tf_op jit(solution)/shard_map/dot_general | solution.py:59
  95.5 8.9 %fusion.7 = f32[1024]{0:T(1024)S(1)} fusion(f32[1024,4096]{1,0:T(8,128)} %get-tuple-element.33, f32[1024]{0:T(1024)S(1)} %max.31), kind=kLoop, calls=%fused_computation.23 | loop fusion | flops 12581888 | bytes 16785408 | tf_op jit(solution)/shard_map/reduce_sum | solution.py:68
  104.4 8.1 %multiply_reduce_fusion.6 = (f32[1024]{0:T(1024)S(1)}, f32[1024,4096]{1,0:T(8,128)}) fusion(bf16[1024,128]{1,0:T(8,128)(2,1)S(1)} %reshape.193, bf16[4096,256]{1,0:T(8,128)(2,1)S(1)} %copy-done), kind=kOutput, calls=%fused_computation.14 | convolution fusion | flops 1082129408 | bytes 18092032 | tf_op jit(solution)/shard_map/dot_general | solution.py:59
  112.7 8.9 %fusion.3 = f32[1024]{0:T(1024)S(1)} fusion(f32[1024,4096]{1,0:T(8,128)} %get-tuple-element.41, f32[1024]{0:T(1024)S(1)} %max.29), kind=kLoop, calls=%fused_computation.19 | loop fusion | flops 12581888 | bytes 16785408 | tf_op jit(solution)/shard_map/reduce_sum | solution.py:68
  121.6 9.7 %fusion.12 = f32[4096,128]{0,1:T(8,128)} fusion(bf16[1024,128]{1,0:T(8,128)(2,1)S(1)} %copy-done.27, f32[1024,4096]{1,0:T(8,128)} %get-tuple-element.33, f32[1024]{0:T(1024)S(1)} %add.109, f32[1024]{0:T(1024)S(1)} %max.31), kind=kOutput, calls=%fused_computation.29 | convolution fusion | flops 1090519040 | bytes 19144704 | tf_op jit(solution)/shard_map/dot_general | solution.py:78
  131.4 0.4 slice-done.3
  131.8 5.2 fusion.16
  137.0 8.1 %multiply_reduce_fusion.7 = (f32[1024]{0:T(1024)S(1)}, f32[1024,4096]{1,0:T(8,128)}) fusion(bf16[1024,128]{1,0:T(8,128)(2,1)S(1)} %reshape.191, bf16[4096,256]{1,0:T(8,128)(2,1)S(1)} %copy-done.1), kind=kOutput, calls=%fused_computation.15 | convolution fusion | flops 1082129408 | bytes 18092032 | tf_op jit(solution)/shard_map/dot_general | solution.py:59
  145.1 8.8 %fusion.1 = f32[1024]{0:T(1024)S(1)} fusion(f32[1024,4096]{1,0:T(8,128)} %get-tuple-element.45, f32[1024]{0:T(1024)S(1)} %max.28), kind=kLoop, calls=%fused_computation.17 | loop fusion | flops 12581888 | bytes 16785408 | tf_op jit(solution)/shard_map/reduce_sum | solution.py:68
  154.0 11.9 %fusion.31 = f32[4096,128]{0,1:T(8,128)} fusion(f32[4096,128]{0,1:T(8,128)} %fusion.12, bf16[1024,128]{1,0:T(8,128)(2,1)} %reshape.196, f32[1024,4096]{1,0:T(8,128)} %get-tuple-element.37, f32[1024]{0:T(1024)S(1)} %add.107, f32[1024]{0:T(1024)S(1)} %max.30), kind=kOutput, calls=%fused_computation.46 | convolution fusion | flops 1091043328 | bytes 21241856 | tf_op jit(solution)/shard_map/dot_general | solution.py:78
  166.5 0.9 fusion.41
  167.4 0.9 fusion.39
  168.3 0.9 fusion.38
  169.3 5.3 fusion.28
  174.6 11.8 %multiply_reduce_fusion.1 = (f32[1024]{0:T(1024)S(1)}, f32[1024,4096]{1,0:T(8,128)}) fusion(f32[1024]{0:T(1024)S(1)} %add.107, f32[1024]{0:T(1024)S(1)} %max.30, f32[1024,4096]{1,0:T(8,128)} %get-tuple-element.37, bf16[1024,128]{1,0:T(8,128)(2,1)S(1)} %copy-done.30, bf16[4096,256]{1,0:T(8,128)(2,1)} %all-gather.6.cloned.1.call-done), kind=kOutput, calls=%fused_computation.4 | convolution fusion | flops 1094712320 | bytes 34877440 | tf_op jit(solution)/shard_map/dot_general | solution.py:71
  186.4 14.7 %fusion.10 = f32[4096,128]{0,1:T(8,128)} fusion(bf16[1024,128]{1,0:T(8,128)(2,1)S(1)} %copy-done.16, f32[1024,4096]{1,0:T(8,128)} %get-tuple-element.49, f32[1024]{0:T(1024)S(1)} %add.108, f32[1024,4096]{1,0:T(8,128)} %get-tuple-element.37, f32[1024]{0:T(1024)S(1)} %add.107, f32[1024]{0:T(1024)S(1)} %max.30), kind=kOutput, calls=%fused_computation.26 | convolution fusion | flops 1098907648 | bytes 35926016 | tf_op jit(solution)/shard_map/dot_general | solution.py:82
  201.1 12.0 %multiply_reduce_fusion = (f32[1024]{0:T(1024)S(1)}, f32[1024,4096]{1,0:T(8,128)}) fusion(f32[1024]{0:T(1024)S(1)} %add.109, f32[1024]{0:T(1024)S(1)} %max.31, f32[1024,4096]{1,0:T(8,128)} %get-tuple-element.33, bf16[1024,128]{1,0:T(8,128)(2,1)S(1)} %copy-done.28, bf16[4096,256]{1,0:T(8,128)(2,1)} %all-gather.6.cloned.1.call-done), kind=kOutput, calls=%fused_computation.1 | convolution fusion | flops 1094712320 | bytes 34877440 | tf_op jit(solution)/shard_map/dot_general | solution.py:71
  213.2 9.3 %multiply_reduce_fusion.3 = (f32[1024]{0:T(1024)S(1)}, f32[1024,4096]{1,0:T(8,128)}) fusion(f32[1024]{0:T(1024)S(1)} %add.102, f32[1024]{0:T(1024)S(1)} %max.28, f32[1024,4096]{1,0:T(8,128)S(1)} %bitcast.34, bf16[1024,128]{1,0:T(8,128)(2,1)S(1)} %copy-done.26, bf16[4096,256]{1,0:T(8,128)(2,1)} %all-gather.6.cloned.1.call-done), kind=kOutput, calls=%fused_computation.10 | convolution fusion | flops 1094712320 | bytes 34877440 | tf_op jit(solution)/shard_map/dot_general | solution.py:71
  222.6 14.7 %fusion.8 = f32[4096,128]{0,1:T(8,128)} fusion(bf16[1024,128]{1,0:T(8,128)(2,1)S(1)} %copy-done.14, f32[1024,4096]{1,0:T(8,128)} %get-tuple-element.53, f32[1024]{0:T(1024)S(1)} %add.103, f32[1024,4096]{1,0:T(8,128)} %get-tuple-element.45, f32[1024]{0:T(1024)S(1)} %add.102, f32[1024]{0:T(1024)S(1)} %max.28), kind=kOutput, calls=%fused_computation.24 | convolution fusion | flops 1098907648 | bytes 35926016 | tf_op jit(solution)/shard_map/dot_general | solution.py:82
  237.3 11.6 %multiply_reduce_fusion.2 = (f32[1024]{0:T(1024)S(1)}, f32[1024,4096]{1,0:T(8,128)}) fusion(f32[1024]{0:T(1024)S(1)} %copy-done.34, f32[1024]{0:T(1024)S(1)} %copy-done.32, f32[1024,4096]{1,0:T(8,128)} %get-tuple-element.41, bf16[1024,128]{1,0:T(8,128)(2,1)S(1)} %copy-done.25, bf16[4096,256]{1,0:T(8,128)(2,1)S(1)} %copy-done.38), kind=kOutput, calls=%fused_computation.7 | convolution fusion | flops 1094712320 | bytes 34877440 | tf_op jit(solution)/shard_map/dot_general | solution.py:71
  249.0 13.7 %fusion.27 = f32[4096,128]{0,1:T(8,128)S(1)} fusion(f32[4096,128]{0,1:T(8,128)S(1)} %copy-done.40, bf16[1024,128]{1,0:T(8,128)(2,1)S(1)} %copy-done.12, f32[1024,4096]{1,0:T(8,128)} %get-tuple-element.51, f32[1024]{0:T(1024)S(1)} %add.110, f32[1024,4096]{1,0:T(8,128)} %get-tuple-element.33, f32[1024]{0:T(1024)S(1)} %add.109, f32[1024]{0:T(1024)S(1)} %max.31), kind=kOutput, calls=%fused_computation.44 | convolution fusion | flops 1099956224 | bytes 38023168 | tf_op jit(solution)/shard_map/dot_general | solution.py:82
  262.7 14.0 %fusion.26 = f32[4096,128]{0,1:T(8,128)S(1)} fusion(f32[4096,128]{0,1:T(8,128)S(1)} %copy-done.41, bf16[1024,128]{1,0:T(8,128)(2,1)S(1)} %copy-done.10, f32[1024,4096]{1,0:T(8,128)} %get-tuple-element.55, f32[1024]{0:T(1024)S(1)} %add.105, f32[1024,4096]{1,0:T(8,128)} %get-tuple-element.41, f32[1024]{0:T(1024)S(1)} %copy-done.34, f32[1024]{0:T(1024)S(1)} %copy-done.32), kind=kOutput, calls=%fused_computation.43 | convolution fusion | flops 1099956224 | bytes 38023168 | tf_op jit(solution)/shard_map/dot_general | solution.py:82
  276.7 3.8 pad_maximum_fusion
  280.6 113.3 %reduce-scatter.2.cloned.1.call-done = f32[512,512]{0,1:T(8,128)} async-done(((f32[4096,512]{0,1:T(8,128)}), f32[512,512]{0,1:T(8,128)}) %reduce-scatter.2.cloned.1.call-update) | async-done | bytes 1048592 | tf_op jit(solution)/shard_map/reduce_scatter | solution.py:19
  393.9 1.3 fusion.87
  396.2 2.3 broadcast_in_dim.31
  398.5 52.2 %all_to_all.6 = f32[4,1,262144]{2,1,0:T(1,128)} all-to-all(f32[4,1,262144]{2,1,0:T(1,128)S(1)} %broadcast_in_dim.31), channel_id=1, replica_groups=mesh['dp'=8,'tensor'=4,'replica'=4] {'replica'}, dimensions={0} | all-to-all | bytes 8388608 | tf_op jit(solution)/shard_map/all_to_all | solution.py:28
  450.7 9.8 %reduce_sum.169 = f32[262144]{0:T(1024)S(1)} reduce(f32[4,1,262144]{2,1,0:T(1,128)} %all_to_all.6, f32[]{:T(128)} %constant.5.clone.1), dimensions={0,1}, to_apply=%region_25.26 | reduce | flops 786432 | bytes 5242884 | tf_op jit(solution)/shard_map/reduce_sum | solution.py:33
  461.0 3.9 fusion.81
  464.9 0.8 pad_maximum_fusion.2
  465.7 67.6 %all-gather.8.cloned.1.call-done = bf16[4096,512]{1,0:T(8,128)(2,1)} async-done(((bf16[512,512]{1,0:T(8,128)(2,1)}), bf16[4096,512]{1,0:T(8,128)(2,1)}) %all-gather.8.cloned.1.call-update) | async-done | bytes 4194320 | tf_op jit(solution)/shard_map/all_gather | solution.py:50
  533.4 4.5 fusion.85
  (153 shorter events, 4.4 us)
Async XLA Ops:
  7.2 17.0 %copy-start.23 = (bf16[256,256]{1,0:T(8,128)(2,1)S(1)}, bf16[256,256]{1,0:T(8,128)(2,1)}, u32[]{:S(2)}) copy-start(bf16[256,256]{1,0:T(8,128)(2,1)} %param.13) | copy-start | bytes 393220
  7.2 61.4 %all-gather.4.cloned.1.call-start = ((), (), s32[]{:S(2)}) async-start(), calls=%async_computation.2 | async-start | bytes 2359296 | tf_op jit(solution)/shard_map/all_gather | solution.py:147
  9.1 165.5 %all-gather.6.cloned.1.call-start = ((), (), s32[]{:S(2)}) async-start(), calls=%async_computation.3 | async-start | bytes 2359296 | tf_op jit(solution)/shard_map/all_gather | solution.py:148
  10.9 383.0 %reduce-scatter.2.cloned.1.call-start = ((), (), s32[]{:S(2)}) async-start(), calls=%async_computation.4 | async-start | bytes 9437184 | tf_op jit(solution)/shard_map/reduce_scatter | solution.py:19
  14.1 122.9 %copy-start.13 = (bf16[1024,128]{1,0:T(8,128)(2,1)}, bf16[1024,128]{1,0:T(8,128)(2,1)S(1)}, u32[]{:S(2)}) copy-start(bf16[1024,128]{1,0:T(8,128)(2,1)S(1)} %reshape.191) | copy-start | bytes 786436
  14.3 90.1 %copy-start.9 = (bf16[1024,128]{1,0:T(8,128)(2,1)}, bf16[1024,128]{1,0:T(8,128)(2,1)S(1)}, u32[]{:S(2)}) copy-start(bf16[1024,128]{1,0:T(8,128)(2,1)S(1)} %reshape.193) | copy-start | bytes 786436
  14.5 72.7 %copy-start.11 = (bf16[1024,128]{1,0:T(8,128)(2,1)}, bf16[1024,128]{1,0:T(8,128)(2,1)S(1)}, u32[]{:S(2)}) copy-start(bf16[1024,128]{1,0:T(8,128)(2,1)S(1)} %reshape.197) | copy-start | bytes 786436
  20.7 66.5 %copy-start.2 = (f32[1024,256]{0,1:T(8,128)}, f32[1024,256]{0,1:T(8,128)S(1)}, u32[]{:S(2)}) copy-start(f32[1024,256]{0,1:T(8,128)S(1)} %get-tuple-element.39) | copy-start | bytes 3145732
  21.9 73.4 %copy-start.4 = (f32[1024,256]{0,1:T(8,128)}, f32[1024,256]{0,1:T(8,128)S(1)}, u32[]{:S(2)}) copy-start(f32[1024,256]{0,1:T(8,128)S(1)} %get-tuple-element.35) | copy-start | bytes 3145732
  68.6 18.6 %copy-start = (bf16[4096,256]{1,0:T(8,128)(2,1)S(1)}, bf16[4096,256]{1,0:T(8,128)(2,1)}, u32[]{:S(2)}) copy-start(bf16[4096,256]{1,0:T(8,128)(2,1)} %all-gather.4.cloned.1.call-done) | copy-start | bytes 6291460
  95.5 17.1 %copy-start.6 = (f32[1024,256]{0,1:T(8,128)S(1)}, f32[1024,256]{0,1:T(8,128)}, u32[]{:S(2)}) copy-start(f32[1024,256]{0,1:T(8,128)} %get-tuple-element.43) | copy-start | bytes 3145732
  104.4 17.2 %copy-start.27 = (bf16[1024,128]{1,0:T(8,128)(2,1)S(1)}, bf16[1024,128]{1,0:T(8,128)(2,1)}, u32[]{:S(2)}) copy-start(bf16[1024,128]{1,0:T(8,128)(2,1)} %reshape.198) | copy-start | bytes 786436
  112.5 54.9 %copy-start.31 = (f32[1024]{0:T(1024)}, f32[1024]{0:T(1024)S(1)}, u32[]{:S(2)}) copy-start(f32[1024]{0:T(1024)S(1)} %max.29) | copy-start | bytes 12292
  112.7 18.7 %slice-start = ((s8[16777216]{0:T(1024)(128)(4,1)}), s8[4194304]{0:T(1024)(128)(4,1)S(1)}, s32[]{:S(2)}) async-start(s8[16777216]{0:T(1024)(128)(4,1)} %bitcast.29), calls=%async_computation.6 | async-start | bytes 8388608
  131.8 35.6 %copy-start.33 = (f32[1024]{0:T(1024)}, f32[1024]{0:T(1024)S(1)}, u32[]{:S(2)}) copy-start(f32[1024]{0:T(1024)S(1)} %add.104) | copy-start | bytes 12292
  145.1 24.1 %slice-start.4 = ((s8[16777216]{0:T(1024)(128)(4,1)}), s8[4194304]{0:T(1024)(128)(4,1)S(1)}, s32[]{:S(2)}) async-start(s8[16777216]{0:T(1024)(128)(4,1)} %bitcast.31), calls=%async_computation.10 | async-start | bytes 8388608
  153.9 12.0 %copy-start.8 = (f32[1024,256]{0,1:T(8,128)S(1)}, f32[1024,256]{0,1:T(8,128)}, u32[]{:S(2)}) copy-start(f32[1024,256]{0,1:T(8,128)} %get-tuple-element.47) | copy-start | bytes 3145732
  153.9 12.2 %copy-start.3 = (f32[1024,256]{0,1:T(8,128)S(1)}, f32[1024,256]{0,1:T(8,128)}, u32[]{:S(2)}) copy-start(f32[1024,256]{0,1:T(8,128)} %copy-done.2) | copy-start | bytes 3145732
  153.9 12.2 %copy-start.29 = (bf16[1024,128]{1,0:T(8,128)(2,1)S(1)}, bf16[1024,128]{1,0:T(8,128)(2,1)}, u32[]{:S(2)}) copy-start(bf16[1024,128]{1,0:T(8,128)(2,1)} %reshape.196) | copy-start | bytes 786436
  153.9 12.2 %copy-start.39 = (bf16[256,256]{1,0:T(8,128)(2,1)S(1)}, bf16[256,256]{1,0:T(8,128)(2,1)}, u32[]{:S(2)}) copy-start(bf16[256,256]{1,0:T(8,128)(2,1)} %param.14) | copy-start | bytes 393220
  153.9 12.5 %copy-start.5 = (f32[1024,256]{0,1:T(8,128)S(1)}, f32[1024,256]{0,1:T(8,128)}, u32[]{:S(2)}) copy-start(f32[1024,256]{0,1:T(8,128)} %copy-done.4) | copy-start | bytes 3145732
  154.0 12.5 %copy-start.28 = (bf16[1024,128]{1,0:T(8,128)(2,1)S(1)}, bf16[1024,128]{1,0:T(8,128)(2,1)}, u32[]{:S(2)}) copy-start(bf16[1024,128]{1,0:T(8,128)(2,1)} %reshape.198) | copy-start | bytes 786436
  154.0 13.4 %copy-start.7 = (f32[1024,256]{0,1:T(8,128)S(1)}, f32[1024,256]{0,1:T(8,128)}, u32[]{:S(2)}) copy-start(f32[1024,256]{0,1:T(8,128)} %get-tuple-element.43) | copy-start | bytes 3145732
  154.0 14.3 %copy-start.26 = (bf16[1024,128]{1,0:T(8,128)(2,1)S(1)}, bf16[1024,128]{1,0:T(8,128)(2,1)}, u32[]{:S(2)}) copy-start(bf16[1024,128]{1,0:T(8,128)(2,1)} %reshape.192) | copy-start | bytes 786436
  154.0 15.2 %slice-start.5 = ((s8[16777216]{0:T(1024)(128)(4,1)}), s8[4194304]{0:T(1024)(128)(4,1)S(1)}, s32[]{:S(2)}) async-start(s8[16777216]{0:T(1024)(128)(4,1)} %bitcast.31), calls=%async_computation.11 | async-start | bytes 8388608
  154.0 15.2 %slice-start.6 = ((s8[16777216]{0:T(1024)(128)(4,1)}), s8[4194304]{0:T(1024)(128)(4,1)S(1)}, s32[]{:S(2)}) async-start(s8[16777216]{0:T(1024)(128)(4,1)} %bitcast.31), calls=%async_computation.12 | async-start | bytes 8388608
  154.0 15.2 %slice-start.7 = ((s8[16777216]{0:T(1024)(128)(4,1)}), s8[4194304]{0:T(1024)(128)(4,1)S(1)}, s32[]{:S(2)}) async-start(s8[16777216]{0:T(1024)(128)(4,1)} %bitcast.31), calls=%async_computation.13 | async-start | bytes 8388608
  174.6 11.8 %copy-start.16 = (bf16[1024,128]{1,0:T(8,128)(2,1)S(1)}, bf16[1024,128]{1,0:T(8,128)(2,1)}, u32[]{:S(2)}) copy-start(bf16[1024,128]{1,0:T(8,128)(2,1)} %copy-done.15) | copy-start | bytes 786436
  186.4 26.8 %slice-start.8 = ((s8[16777216]{0:T(1024)(128)(4,1)}), s8[4194304]{0:T(1024)(128)(4,1)S(1)}, s32[]{:S(2)}) async-start(s8[16777216]{0:T(1024)(128)(4,1)} %bitcast.33), calls=%async_computation.14 | async-start | bytes 8388608
  186.4 26.8 %slice-start.9 = ((s8[16777216]{0:T(1024)(128)(4,1)}), s8[4194304]{0:T(1024)(128)(4,1)S(1)}, s32[]{:S(2)}) async-start(s8[16777216]{0:T(1024)(128)(4,1)} %bitcast.33), calls=%async_computation.15 | async-start | bytes 8388608
  186.4 26.8 %slice-start.10 = ((s8[16777216]{0:T(1024)(128)(4,1)}), s8[4194304]{0:T(1024)(128)(4,1)S(1)}, s32[]{:S(2)}) async-start(s8[16777216]{0:T(1024)(128)(4,1)} %bitcast.33), calls=%async_computation.16 | async-start | bytes 8388608
  201.1 12.0 %copy-start.37 = (f32[1024]{0:T(1024)S(1)}, f32[1024]{0:T(1024)}, u32[]{:S(2)}) copy-start(f32[1024]{0:T(1024)} %fusion.41) | copy-start | bytes 12292
  201.1 12.1 %slice-start.11 = ((s8[16777216]{0:T(1024)(128)(4,1)}), s8[4194304]{0:T(1024)(128)(4,1)S(1)}, s32[]{:S(2)}) async-start(s8[16777216]{0:T(1024)(128)(4,1)} %bitcast.33), calls=%async_computation.17 | async-start | bytes 8388608
  222.5 14.8 %copy-start.25 = (bf16[1024,128]{1,0:T(8,128)(2,1)S(1)}, bf16[1024,128]{1,0:T(8,128)(2,1)}, u32[]{:S(2)}) copy-start(bf16[1024,128]{1,0:T(8,128)(2,1)} %reshape.194) | copy-start | bytes 786436
  222.5 14.7 %copy-start.32 = (f32[1024]{0:T(1024)S(1)}, f32[1024]{0:T(1024)}, u32[]{:S(2)}) copy-start(f32[1024]{0:T(1024)} %copy-done.31) | copy-start | bytes 12292
  222.6 14.7 %copy-start.34 = (f32[1024]{0:T(1024)S(1)}, f32[1024]{0:T(1024)}, u32[]{:S(2)}) copy-start(f32[1024]{0:T(1024)} %copy-done.33) | copy-start | bytes 12292
  222.6 14.7 %copy-start.38 = (bf16[4096,256]{1,0:T(8,128)(2,1)S(1)}, bf16[4096,256]{1,0:T(8,128)(2,1)}, u32[]{:S(2)}) copy-start(bf16[4096,256]{1,0:T(8,128)(2,1)} %all-gather.6.cloned.1.call-done) | copy-start | bytes 6291460
  237.3 11.7 %copy-start.35 = (f32[1024]{0:T(1024)S(1)}, f32[1024]{0:T(1024)}, u32[]{:S(2)}) copy-start(f32[1024]{0:T(1024)} %fusion.39) | copy-start | bytes 12292
  237.3 11.7 %copy-start.12 = (bf16[1024,128]{1,0:T(8,128)(2,1)S(1)}, bf16[1024,128]{1,0:T(8,128)(2,1)}, u32[]{:S(2)}) copy-start(bf16[1024,128]{1,0:T(8,128)(2,1)} %copy-done.11) | copy-start | bytes 786436
  249.0 13.7 %copy-start.10 = (bf16[1024,128]{1,0:T(8,128)(2,1)S(1)}, bf16[1024,128]{1,0:T(8,128)(2,1)}, u32[]{:S(2)}) copy-start(bf16[1024,128]{1,0:T(8,128)(2,1)} %copy-done.9) | copy-start | bytes 786436
  249.0 13.7 %copy-start.41 = (f32[4096,128]{0,1:T(8,128)S(1)}, f32[4096,128]{0,1:T(8,128)}, u32[]{:S(2)}) copy-start(f32[4096,128]{0,1:T(8,128)} %fusion.8) | copy-start | bytes 6291460
  262.7 14.0 %copy-start.17 = (f32[4096,128]{0,1:T(8,128)S(1)}, f32[4096,128]{0,1:T(8,128)}, u32[]{:S(2)}) copy-start(f32[4096,128]{0,1:T(8,128)} %fusion.31) | copy-start | bytes 6291460
  262.7 14.0 %copy-start.18 = (f32[4096,128]{0,1:T(8,128)S(1)}, f32[4096,128]{0,1:T(8,128)}, u32[]{:S(2)}) copy-start(f32[4096,128]{0,1:T(8,128)} %fusion.28) | copy-start | bytes 6291460
  280.5 180.4 %copy-start.19 = (f32[512,256]{1,0:T(8,128)S(1)}, f32[512,256]{1,0:T(8,128)}, u32[]{:S(2)}) copy-start(f32[512,256]{1,0:T(8,128)} %param.16) | copy-start | bytes 1572868
  280.5 180.4 %copy-start.20 = (f32[512,256]{1,0:T(8,128)S(1)}, f32[512,256]{1,0:T(8,128)}, u32[]{:S(2)}) copy-start(f32[512,256]{1,0:T(8,128)} %param.17) | copy-start | bytes 1572868
  280.5 252.8 %all-gather.8.cloned.1.call-start = ((), (), s32[]{:S(2)}) async-start(), calls=%async_computation.5 | async-start | bytes 4718592 | tf_op jit(solution)/shard_map/all_gather | solution.py:50
  460.8 77.1 %copy-start.21 = (f32[512,256]{1,0:T(8,128)}, f32[512,256]{1,0:T(8,128)S(1)}, u32[]{:S(2)}) copy-start(f32[512,256]{1,0:T(8,128)S(1)} %slice.109) | copy-start | bytes 1572868
  461.0 76.9 %copy-start.22 = (f32[512,256]{1,0:T(8,128)}, f32[512,256]{1,0:T(8,128)S(1)}, u32[]{:S(2)}) copy-start(f32[512,256]{1,0:T(8,128)S(1)} %slice.107) | copy-start | bytes 1572868
  (11 other events, 88.9 us)
Sparse Core Ops, SparseCore 0:
  10.9 57.6 all-gather.3
  71.5 53.7 all-gather.5
  280.6 113.2 reduce-scatter.1
  465.8 67.4 all-gather.7
where the time goes:
time: 554 us; the launch traced here: 545 us
  waiting for transfers between devices  224 us (40%)
  matrix products  177 us (32%)
  other arithmetic  59 us (11%)
  blocking collectives  52.2 us (9%)
  local copies, waits for them, and re-layouts  17.6 us (3%)
  between operations  15 us (3%)
    reduce_scatter x1, waiting for transfers between devices, sent_together(): lax.psum_scatter(both, axis, scatter_dimension=dim, tiled=True)  113 us
    all_gather x1, waiting for transfers between devices, side_by_side(): lax.all_gather(both, axis, axis=dim, tiled=True)  67.6 us
    dot_general x4, matrix products, attend_block(): lax.dot_general(cart_dscore, flat_query, contract, preferred_element_type...  57.1 us
    all_to_all x1, blocking collectives, from_everyone(): return lax.all_to_all(copies, axis, split_axis=0, concat_axis=0, tiled=True)  52.2 us
    dot_general x4, matrix products, attend_block(): jnp.dot(flat_grad, cart_values.T, preferred_element_type=jnp.float32)  44.7 us
    all_gather x1, waiting for transfers between devices, per_device(): lax.all_gather(master_keys.astype(jnp.bfloat16), 'dp', axis=0, tiled=True)  43.1 us
    reduce_sum x4, other arithmetic, attend_block(): jnp.sum(cart_exp, axis=1, keepdims=True)  35.5 us
    dot_general x4, matrix products, attend_block(): jnp.dot(flat_query, cart_keys.T, preferred_element_type=jnp.float32)  33.8 us
  transfers between devices with their start and end apart: 4, of which 3 were waited for; matrix products, arithmetic and copies ran while one was open for 22% of the time, Pallas kernels for 0%

commit v1 on v0

--- a/solution.py
+++ b/solution.py
@@ -144,7 +144,12 @@
     second_values,
 ):
     cart_keys, cart_values = (
-        lax.all_gather(master_keys.astype(jnp.bfloat16), "dp", axis=0, tiled=True),
+        jnp.concatenate(
+            lax.all_to_all(
+                jnp.stack([master_keys.astype(jnp.bfloat16)] * lax.axis_size("dp")), "dp", 0, 0
+            ),
+            axis=0,
+        ),
         lax.all_gather(master_values.astype(jnp.bfloat16), "dp", axis=0, tiled=True),
     )
     grad_keys, grad_values = device_grads(

time: 554 us -> 537 us (0.969)
  waiting for transfers between devices: 224 us -> 188 us
  local copies, waits for them, and re-layouts: 17.6 us -> 26.5 us
  starting transfers between devices: 0.16 us -> 8.02 us
    all_gather x1 -> x0, waiting for transfers between devices: 43.1 us -> none  [per_device(): lax.all_gather(master_keys.astype(jnp.bfloat16), 'dp', axis=0, tiled=True)]
    all_to_all x0 -> x1, starting transfers between devices: none -> 7.89 us  [per_device(): lax.all_to_all(jnp.stack([master_keys.astype(jnp.bfloat16)] * lax.axis_si...]
  transfers between devices with their start and end apart: 4 -> 4, of which waited for: 3 -> 3; matrix products, arithmetic and copies ran while one was open for 22% -> 25% of each run, Pallas kernels for 0% -> 0%
where the time goes in v1:
time: 537 us; the launch traced here: 527 us
  waiting for transfers between devices  188 us (35%)
  matrix products  179 us (33%)
  other arithmetic  58.9 us (11%)
  blocking collectives  52.2 us (10%)
  local copies, waits for them, and re-layouts  26.5 us (5%)
  between operations  14.7 us (3%)
  starting transfers between devices  8.02 us (1%)
    reduce_scatter x1, waiting for transfers between devices, sent_together(): lax.psum_scatter(both, axis, scatter_dimension=dim, tiled=True)  116 us
    all_gather x1, waiting for transfers between devices, side_by_side(): lax.all_gather(both, axis, axis=dim, tiled=True)  67.6 us
    dot_general x4, matrix products, attend_block(): lax.dot_general(cart_dscore, flat_query, contract, preferred_element_type...  57.3 us
    all_to_all x1, blocking collectives, from_everyone(): return lax.all_to_all(copies, axis, split_axis=0, concat_axis=0, tiled=True)  52.2 us
    dot_general x4, matrix products, attend_block(): jnp.dot(flat_grad, cart_values.T, preferred_element_type=jnp.float32)  44.5 us
    reduce_sum x4, other arithmetic, attend_block(): jnp.sum(cart_exp, axis=1, keepdims=True)  34.9 us
    dot_general x4, matrix products, attend_block(): jnp.dot(flat_query, cart_keys.T, preferred_element_type=jnp.float32)  33.9 us
    dot_general x4, matrix products, attend_block(): lax.dot_general(cart_probs.astype(jnp.bfloat16), flat_grad, contract, pre...  31.9 us
  transfers between devices with their start and end apart: 4, of which 3 were waited for; matrix products, arithmetic and copies ran while one was open for 25% of the time, Pallas kernels for 0%

profile of v1, /device:TPU:0, one launch (start us, length us, event | category | flops | bytes accessed | tf_op | source)
XLA Modules:
  0.0 527.1 jit_solution(4726103808294323209)
XLA Ops:
  7.2 1.1 convert_element_type.36
  8.3 1.5 stack.2
  9.8 7.9 %all-to-all-start = ((bf16[8,512,256]{2,1,0:T(8,128)(2,1)}), bf16[8,512,256]{2,1,0:T(8,128)(2,1)S(1)}, u32[]{:S(2)}, u32[]{:S(2)}) async-start(bf16[8,512,256]{2,1,0:T(8,128)(2,1)} %stack.2), calls=%async_computation | async-start | bytes 4194304 | tf_op jit(solution)/shard_map/all_to_all | solution.py:148
  17.7 1.8 convert_element_type.37
  19.5 2.0 fusion.89
  21.5 0.9 reshape.204
  22.4 2.1 fusion.88
  27.0 1.8 reshape.202
  28.8 1.8 reshape.201
  31.5 1.8 reshape.199
  35.1 1.3 fusion.90
  36.4 2.5 fusion.91
  38.8 2.3 fusion.92
  41.1 2.3 fusion.93
  43.4 4.5 all-to-all-done
  47.8 9.1 %multiply_reduce_fusion.4 = (f32[1024]{0:T(1024)S(1)}, f32[1024,4096]{1,0:T(8,128)}) fusion(bf16[1024,128]{1,0:T(8,128)(2,1)} %reshape.203, bf16[4096,256]{1,0:T(8,128)(2,1)S(1)} %bitcast.36), kind=kOutput, calls=%fused_computation.12 | convolution fusion | flops 1082129408 | bytes 18092032 | tf_op jit(solution)/shard_map/dot_general | solution.py:59
  56.9 8.2 %multiply_reduce_fusion.5 = (f32[1024]{0:T(1024)S(1)}, f32[1024,4096]{1,0:T(8,128)}) fusion(bf16[1024,128]{1,0:T(8,128)(2,1)S(1)} %copy-done.11, bf16[4096,256]{1,0:T(8,128)(2,1)S(1)} %bitcast.37), kind=kOutput, calls=%fused_computation.13 | convolution fusion | flops 1082129408 | bytes 18092032 | tf_op jit(solution)/shard_map/dot_general | solution.py:59
  65.1 8.1 %multiply_reduce_fusion.6 = (f32[1024]{0:T(1024)S(1)}, f32[1024,4096]{1,0:T(8,128)}) fusion(bf16[1024,128]{1,0:T(8,128)(2,1)S(1)} %copy-done.7, bf16[4096,256]{1,0:T(8,128)(2,1)S(1)} %bitcast.38), kind=kOutput, calls=%fused_computation.14 | convolution fusion | flops 1082129408 | bytes 18092032 | tf_op jit(solution)/shard_map/dot_general | solution.py:59
  73.2 8.6 %multiply_reduce_fusion.7 = (f32[1024]{0:T(1024)S(1)}, f32[1024,4096]{1,0:T(8,128)}) fusion(bf16[1024,128]{1,0:T(8,128)(2,1)S(1)} %copy-done.9, bf16[4096,256]{1,0:T(8,128)(2,1)S(1)} %bitcast.39), kind=kOutput, calls=%fused_computation.15 | convolution fusion | flops 1082129408 | bytes 18092032 | tf_op jit(solution)/shard_map/dot_general | solution.py:59
  81.7 8.7 %fusion.7 = f32[1024]{0:T(1024)S(1)} fusion(f32[1024,4096]{1,0:T(8,128)} %get-tuple-element.33, f32[1024]{0:T(1024)S(1)} %max.31), kind=kLoop, calls=%fused_computation.23 | loop fusion | flops 12581888 | bytes 16785408 | tf_op jit(solution)/shard_map/reduce_sum | solution.py:68
  90.7 8.7 %fusion.5 = f32[1024]{0:T(1024)S(1)} fusion(f32[1024,4096]{1,0:T(8,128)} %get-tuple-element.37, f32[1024]{0:T(1024)S(1)} %max.30), kind=kLoop, calls=%fused_computation.21 | loop fusion | flops 12581888 | bytes 16785408 | tf_op jit(solution)/shard_map/reduce_sum | solution.py:68
  99.5 8.8 %fusion.3 = f32[1024]{0:T(1024)S(1)} fusion(f32[1024,4096]{1,0:T(8,128)} %get-tuple-element.41, f32[1024]{0:T(1024)S(1)} %max.29), kind=kLoop, calls=%fused_computation.19 | loop fusion | flops 12581888 | bytes 16785408 | tf_op jit(solution)/shard_map/reduce_sum | solution.py:68
  108.3 1.4 fusion.43
  109.8 9.5 %fusion.12 = f32[4096,128]{0,1:T(8,128)} fusion(bf16[1024,128]{1,0:T(8,128)(2,1)S(1)} %copy-done.22, f32[1024,4096]{1,0:T(8,128)} %get-tuple-element.33, f32[1024]{0:T(1024)S(1)} %add.109, f32[1024]{0:T(1024)S(1)} %max.31), kind=kOutput, calls=%fused_computation.29 | convolution fusion | flops 1090519040 | bytes 19144704 | tf_op jit(solution)/shard_map/dot_general | solution.py:78
  119.9 5.2 fusion.16
  125.1 8.8 %fusion.1 = f32[1024]{0:T(1024)S(1)} fusion(f32[1024,4096]{1,0:T(8,128)} %get-tuple-element.45, f32[1024]{0:T(1024)S(1)} %max.28), kind=kLoop, calls=%fused_computation.17 | loop fusion | flops 12581888 | bytes 16785408 | tf_op jit(solution)/shard_map/reduce_sum | solution.py:68
  134.0 11.7 %fusion.31 = f32[4096,128]{0,1:T(8,128)} fusion(f32[4096,128]{0,1:T(8,128)} %fusion.12, bf16[1024,128]{1,0:T(8,128)(2,1)} %reshape.202, f32[1024,4096]{1,0:T(8,128)} %get-tuple-element.37, f32[1024]{0:T(1024)S(1)} %add.107, f32[1024]{0:T(1024)S(1)} %max.30), kind=kOutput, calls=%fused_computation.46 | convolution fusion | flops 1091043328 | bytes 21241856 | tf_op jit(solution)/shard_map/dot_general | solution.py:78
  146.3 0.9 fusion.41
  147.2 0.9 fusion.39
  148.1 0.9 fusion.38
  149.1 5.5 %fusion.28 = f32[4096,128]{0,1:T(8,128)} fusion(f32[4096,128]{0,1:T(8,128)S(1)} %copy-done.37, bf16[1024,128]{1,0:T(8,128)(2,1)S(1)} %copy-done.23, f32[1024,4096]{1,0:T(8,128)S(1)} %bitcast.33, f32[1024]{0:T(1024)S(1)} %add.102, f32[1024]{0:T(1024)S(1)} %max.28), kind=kOutput, calls=%fused_computation.45 | convolution fusion | flops 1091043328 | bytes 21241856 | tf_op jit(solution)/shard_map/dot_general | solution.py:78
  154.6 11.8 %multiply_reduce_fusion.1 = (f32[1024]{0:T(1024)S(1)}, f32[1024,4096]{1,0:T(8,128)}) fusion(f32[1024]{0:T(1024)S(1)} %add.107, f32[1024]{0:T(1024)S(1)} %max.30, f32[1024,4096]{1,0:T(8,128)} %get-tuple-element.37, bf16[1024,128]{1,0:T(8,128)(2,1)S(1)} %copy-done.25, bf16[4096,256]{1,0:T(8,128)(2,1)} %all-gather.3.cloned.1.call-done), kind=kOutput, calls=%fused_computation.4 | convolution fusion | flops 1094712320 | bytes 34877440 | tf_op jit(solution)/shard_map/dot_general | solution.py:71
  166.4 14.7 %fusion.10 = f32[4096,128]{0,1:T(8,128)} fusion(bf16[1024,128]{1,0:T(8,128)(2,1)S(1)} %copy-done.12, f32[1024,4096]{1,0:T(8,128)} %get-tuple-element.49, f32[1024]{0:T(1024)S(1)} %add.108, f32[1024,4096]{1,0:T(8,128)} %get-tuple-element.37, f32[1024]{0:T(1024)S(1)} %add.107, f32[1024]{0:T(1024)S(1)} %max.30), kind=kOutput, calls=%fused_computation.26 | convolution fusion | flops 1098907648 | bytes 35926016 | tf_op jit(solution)/shard_map/dot_general | solution.py:82
  181.1 11.8 %multiply_reduce_fusion = (f32[1024]{0:T(1024)S(1)}, f32[1024,4096]{1,0:T(8,128)}) fusion(f32[1024]{0:T(1024)S(1)} %add.109, f32[1024]{0:T(1024)S(1)} %max.31, f32[1024,4096]{1,0:T(8,128)} %get-tuple-element.33, bf16[1024,128]{1,0:T(8,128)(2,1)S(1)} %copy-done.22, bf16[4096,256]{1,0:T(8,128)(2,1)} %all-gather.3.cloned.1.call-done), kind=kOutput, calls=%fused_computation.1 | convolution fusion | flops 1094712320 | bytes 34877440 | tf_op jit(solution)/shard_map/dot_general | solution.py:71
  193.0 9.3 %multiply_reduce_fusion.3 = (f32[1024]{0:T(1024)S(1)}, f32[1024,4096]{1,0:T(8,128)}) fusion(f32[1024]{0:T(1024)S(1)} %add.102, f32[1024]{0:T(1024)S(1)} %max.28, f32[1024,4096]{1,0:T(8,128)S(1)} %bitcast.35, bf16[1024,128]{1,0:T(8,128)(2,1)S(1)} %copy-done.23, bf16[4096,256]{1,0:T(8,128)(2,1)} %all-gather.3.cloned.1.call-done), kind=kOutput, calls=%fused_computation.10 | convolution fusion | flops 1094712320 | bytes 34877440 | tf_op jit(solution)/shard_map/dot_general | solution.py:71
  202.3 15.2 %fusion.8 = f32[4096,128]{0,1:T(8,128)} fusion(bf16[1024,128]{1,0:T(8,128)(2,1)S(1)} %copy-done.10, f32[1024,4096]{1,0:T(8,128)} %get-tuple-element.53, f32[1024]{0:T(1024)S(1)} %add.103, f32[1024,4096]{1,0:T(8,128)} %get-tuple-element.45, f32[1024]{0:T(1024)S(1)} %add.102, f32[1024]{0:T(1024)S(1)} %max.28), kind=kOutput, calls=%fused_computation.24 | convolution fusion | flops 1098907648 | bytes 35926016 | tf_op jit(solution)/shard_map/dot_general | solution.py:82
  217.6 11.6 %multiply_reduce_fusion.2 = (f32[1024]{0:T(1024)S(1)}, f32[1024,4096]{1,0:T(8,128)}) fusion(f32[1024]{0:T(1024)S(1)} %copy-done.29, f32[1024]{0:T(1024)S(1)} %copy-done.27, f32[1024,4096]{1,0:T(8,128)} %get-tuple-element.41, bf16[1024,128]{1,0:T(8,128)(2,1)S(1)} %copy-done.21, bf16[4096,256]{1,0:T(8,128)(2,1)S(1)} %copy-done.33), kind=kOutput, calls=%fused_computation.7 | convolution fusion | flops 1094712320 | bytes 34877440 | tf_op jit(solution)/shard_map/dot_general | solution.py:71
  229.3 13.7 %fusion.27 = f32[4096,128]{0,1:T(8,128)S(1)} fusion(f32[4096,128]{0,1:T(8,128)S(1)} %copy-done.35, bf16[1024,128]{1,0:T(8,128)(2,1)S(1)} %copy-done.6, f32[1024,4096]{1,0:T(8,128)} %get-tuple-element.51, f32[1024]{0:T(1024)S(1)} %add.110, f32[1024,4096]{1,0:T(8,128)} %get-tuple-element.33, f32[1024]{0:T(1024)S(1)} %add.109, f32[1024]{0:T(1024)S(1)} %max.31), kind=kOutput, calls=%fused_computation.44 | convolution fusion | flops 1099956224 | bytes 38023168 | tf_op jit(solution)/shard_map/dot_general | solution.py:82
  243.0 13.7 %fusion.26 = f32[4096,128]{0,1:T(8,128)S(1)} fusion(f32[4096,128]{0,1:T(8,128)S(1)} %copy-done.36, bf16[1024,128]{1,0:T(8,128)(2,1)S(1)} %copy-done.8, f32[1024,4096]{1,0:T(8,128)} %get-tuple-element.55, f32[1024]{0:T(1024)S(1)} %add.105, f32[1024,4096]{1,0:T(8,128)} %get-tuple-element.41, f32[1024]{0:T(1024)S(1)} %copy-done.29, f32[1024]{0:T(1024)S(1)} %copy-done.27), kind=kOutput, calls=%fused_computation.43 | convolution fusion | flops 1099956224 | bytes 38023168 | tf_op jit(solution)/shard_map/dot_general | solution.py:82
  256.7 3.7 pad_maximum_fusion
  260.5 115.7 %reduce-scatter.2.cloned.1.call-done = f32[512,512]{0,1:T(8,128)} async-done(((f32[4096,512]{0,1:T(8,128)}), f32[512,512]{0,1:T(8,128)}) %reduce-scatter.2.cloned.1.call-update) | async-done | bytes 1048592 | tf_op jit(solution)/shard_map/reduce_scatter | solution.py:19
  376.2 1.3 fusion.87
  378.6 2.5 broadcast_in_dim.31
  381.0 52.2 %all_to_all.11 = f32[4,1,262144]{2,1,0:T(1,128)} all-to-all(f32[4,1,262144]{2,1,0:T(1,128)S(1)} %broadcast_in_dim.31), channel_id=1, replica_groups=mesh['dp'=8,'tensor'=4,'replica'=4] {'replica'}, dimensions={0} | all-to-all | bytes 8388608 | tf_op jit(solution)/shard_map/all_to_all | solution.py:28
  433.3 9.8 %reduce_sum.169 = f32[262144]{0:T(1024)S(1)} reduce(f32[4,1,262144]{2,1,0:T(1,128)} %all_to_all.11, f32[]{:T(128)} %constant.5.clone.1), dimensions={0,1}, to_apply=%region_25.26 | reduce | flops 786432 | bytes 5242884 | tf_op jit(solution)/shard_map/reduce_sum | solution.py:33
  443.5 3.9 fusion.81
  448.2 67.6 %all-gather.5.cloned.1.call-done = bf16[4096,512]{1,0:T(8,128)(2,1)} async-done(((bf16[512,512]{1,0:T(8,128)(2,1)}), bf16[4096,512]{1,0:T(8,128)(2,1)}) %all-gather.5.cloned.1.call-update) | async-done | bytes 4194320 | tf_op jit(solution)/shard_map/all_gather | solution.py:50
  515.9 4.5 fusion.85
  (143 shorter events, 9.3 us)
Async XLA Ops:
  7.2 27.9 %copy-start.19 = (bf16[256,256]{1,0:T(8,128)(2,1)S(1)}, bf16[256,256]{1,0:T(8,128)(2,1)}, u32[]{:S(2)}) copy-start(bf16[256,256]{1,0:T(8,128)(2,1)} %param.13) | copy-start | bytes 393220
  9.8 38.1 %all-to-all-start = ((bf16[8,512,256]{2,1,0:T(8,128)(2,1)}), bf16[8,512,256]{2,1,0:T(8,128)(2,1)S(1)}, u32[]{:S(2)}, u32[]{:S(2)}) async-start(bf16[8,512,256]{2,1,0:T(8,128)(2,1)} %stack.2), calls=%async_computation | async-start | bytes 4194304 | tf_op jit(solution)/shard_map/all_to_all | solution.py:148
  17.6 136.9 %all-gather.3.cloned.1.call-start = ((), (), s32[]{:S(2)}) async-start(), calls=%async_computation.3 | async-start | bytes 2359296 | tf_op jit(solution)/shard_map/all_gather | solution.py:153
  19.5 356.8 %reduce-scatter.2.cloned.1.call-start = ((), (), s32[]{:S(2)}) async-start(), calls=%async_computation.4 | async-start | bytes 9437184 | tf_op jit(solution)/shard_map/reduce_scatter | solution.py:19
  36.3 54.1 %copy-start = (f32[1024,256]{0,1:T(8,128)}, f32[1024,256]{0,1:T(8,128)S(1)}, u32[]{:S(2)}) copy-start(f32[1024,256]{0,1:T(8,128)S(1)} %get-tuple-element.35) | copy-start | bytes 3145732
  47.8 17.3 %copy-start.7 = (bf16[1024,128]{1,0:T(8,128)(2,1)S(1)}, bf16[1024,128]{1,0:T(8,128)(2,1)}, u32[]{:S(2)}) copy-start(bf16[1024,128]{1,0:T(8,128)(2,1)} %reshape.199) | copy-start | bytes 786436
  56.9 16.2 %copy-start.9 = (bf16[1024,128]{1,0:T(8,128)(2,1)S(1)}, bf16[1024,128]{1,0:T(8,128)(2,1)}, u32[]{:S(2)}) copy-start(bf16[1024,128]{1,0:T(8,128)(2,1)} %reshape.196) | copy-start | bytes 786436
  81.7 17.6 %copy-start.3 = (f32[1024,256]{0,1:T(8,128)S(1)}, f32[1024,256]{0,1:T(8,128)}, u32[]{:S(2)}) copy-start(f32[1024,256]{0,1:T(8,128)} %get-tuple-element.39) | copy-start | bytes 3145732
  90.6 19.1 %copy-start.22 = (bf16[1024,128]{1,0:T(8,128)(2,1)S(1)}, bf16[1024,128]{1,0:T(8,128)(2,1)}, u32[]{:S(2)}) copy-start(bf16[1024,128]{1,0:T(8,128)(2,1)} %reshape.204) | copy-start | bytes 786436
  99.5 47.7 %copy-start.26 = (f32[1024]{0:T(1024)}, f32[1024]{0:T(1024)S(1)}, u32[]{:S(2)}) copy-start(f32[1024]{0:T(1024)S(1)} %max.29) | copy-start | bytes 12292
  99.5 19.7 %slice-start = ((s8[16777216]{0:T(1024)(128)(4,1)}), s8[4194304]{0:T(1024)(128)(4,1)S(1)}, s32[]{:S(2)}) async-start(s8[16777216]{0:T(1024)(128)(4,1)} %bitcast.30), calls=%async_computation.6 | async-start | bytes 8388608
  109.7 9.5 %slice-start.1 = ((s8[16777216]{0:T(1024)(128)(4,1)}), s8[4194304]{0:T(1024)(128)(4,1)S(1)}, s32[]{:S(2)}) async-start(s8[16777216]{0:T(1024)(128)(4,1)} %bitcast.30), calls=%async_computation.7 | async-start | bytes 8388608
  109.8 10.2 %slice-start.3 = ((s8[16777216]{0:T(1024)(128)(4,1)}), s8[4194304]{0:T(1024)(128)(4,1)S(1)}, s32[]{:S(2)}) async-start(s8[16777216]{0:T(1024)(128)(4,1)} %bitcast.30), calls=%async_computation.9 | async-start | bytes 8388608
  109.8 10.2 %copy-start.20 = (bf16[1024,128]{1,0:T(8,128)(2,1)S(1)}, bf16[1024,128]{1,0:T(8,128)(2,1)}, u32[]{:S(2)}) copy-start(bf16[1024,128]{1,0:T(8,128)(2,1)} %reshape.200) | copy-start | bytes 786436
  119.9 27.3 %copy-start.28 = (f32[1024]{0:T(1024)}, f32[1024]{0:T(1024)S(1)}, u32[]{:S(2)}) copy-start(f32[1024]{0:T(1024)S(1)} %add.104) | copy-start | bytes 12292
  125.1 23.9 %slice-start.4 = ((s8[16777216]{0:T(1024)(128)(4,1)}), s8[4194304]{0:T(1024)(128)(4,1)S(1)}, s32[]{:S(2)}) async-start(s8[16777216]{0:T(1024)(128)(4,1)} %bitcast.32), calls=%async_computation.10 | async-start | bytes 8388608
  133.9 11.9 %copy-start.5 = (f32[1024,256]{0,1:T(8,128)S(1)}, f32[1024,256]{0,1:T(8,128)}, u32[]{:S(2)}) copy-start(f32[1024,256]{0,1:T(8,128)} %get-tuple-element.47) | copy-start | bytes 3145732
  133.9 12.0 %copy-start.4 = (f32[1024,256]{0,1:T(8,128)S(1)}, f32[1024,256]{0,1:T(8,128)}, u32[]{:S(2)}) copy-start(f32[1024,256]{0,1:T(8,128)} %get-tuple-element.39) | copy-start | bytes 3145732
  133.9 12.0 %copy-start.24 = (bf16[1024,128]{1,0:T(8,128)(2,1)S(1)}, bf16[1024,128]{1,0:T(8,128)(2,1)}, u32[]{:S(2)}) copy-start(bf16[1024,128]{1,0:T(8,128)(2,1)} %reshape.202) | copy-start | bytes 786436
  133.9 12.0 %copy-start.34 = (bf16[256,256]{1,0:T(8,128)(2,1)S(1)}, bf16[256,256]{1,0:T(8,128)(2,1)}, u32[]{:S(2)}) copy-start(bf16[256,256]{1,0:T(8,128)(2,1)} %param.14) | copy-start | bytes 393220
  133.9 12.3 %copy-start.1 = (f32[1024,256]{0,1:T(8,128)S(1)}, f32[1024,256]{0,1:T(8,128)}, u32[]{:S(2)}) copy-start(f32[1024,256]{0,1:T(8,128)} %copy-done) | copy-start | bytes 3145732
  133.9 13.3 %copy-start.2 = (f32[1024,256]{0,1:T(8,128)S(1)}, f32[1024,256]{0,1:T(8,128)}, u32[]{:S(2)}) copy-start(f32[1024,256]{0,1:T(8,128)} %get-tuple-element.43) | copy-start | bytes 3145732
  134.0 14.2 %copy-start.23 = (bf16[1024,128]{1,0:T(8,128)(2,1)S(1)}, bf16[1024,128]{1,0:T(8,128)(2,1)}, u32[]{:S(2)}) copy-start(bf16[1024,128]{1,0:T(8,128)(2,1)} %reshape.198) | copy-start | bytes 786436
  134.0 15.1 %slice-start.5 = ((s8[16777216]{0:T(1024)(128)(4,1)}), s8[4194304]{0:T(1024)(128)(4,1)S(1)}, s32[]{:S(2)}) async-start(s8[16777216]{0:T(1024)(128)(4,1)} %bitcast.32), calls=%async_computation.11 | async-start | bytes 8388608
  134.0 15.1 %slice-start.6 = ((s8[16777216]{0:T(1024)(128)(4,1)}), s8[4194304]{0:T(1024)(128)(4,1)S(1)}, s32[]{:S(2)}) async-start(s8[16777216]{0:T(1024)(128)(4,1)} %bitcast.32), calls=%async_computation.12 | async-start | bytes 8388608
  134.0 15.1 %slice-start.7 = ((s8[16777216]{0:T(1024)(128)(4,1)}), s8[4194304]{0:T(1024)(128)(4,1)S(1)}, s32[]{:S(2)}) async-start(s8[16777216]{0:T(1024)(128)(4,1)} %bitcast.32), calls=%async_computation.13 | async-start | bytes 8388608
  154.6 11.8 %copy-start.12 = (bf16[1024,128]{1,0:T(8,128)(2,1)S(1)}, bf16[1024,128]{1,0:T(8,128)(2,1)}, u32[]{:S(2)}) copy-start(bf16[1024,128]{1,0:T(8,128)(2,1)} %reshape.201) | copy-start | bytes 786436
  166.4 26.6 %slice-start.8 = ((s8[16777216]{0:T(1024)(128)(4,1)}), s8[4194304]{0:T(1024)(128)(4,1)S(1)}, s32[]{:S(2)}) async-start(s8[16777216]{0:T(1024)(128)(4,1)} %bitcast.34), calls=%async_computation.14 | async-start | bytes 8388608
  166.4 26.6 %slice-start.9 = ((s8[16777216]{0:T(1024)(128)(4,1)}), s8[4194304]{0:T(1024)(128)(4,1)S(1)}, s32[]{:S(2)}) async-start(s8[16777216]{0:T(1024)(128)(4,1)} %bitcast.34), calls=%async_computation.15 | async-start | bytes 8388608
  166.4 26.6 %slice-start.10 = ((s8[16777216]{0:T(1024)(128)(4,1)}), s8[4194304]{0:T(1024)(128)(4,1)S(1)}, s32[]{:S(2)}) async-start(s8[16777216]{0:T(1024)(128)(4,1)} %bitcast.34), calls=%async_computation.16 | async-start | bytes 8388608
  181.1 11.8 %copy-start.32 = (f32[1024]{0:T(1024)S(1)}, f32[1024]{0:T(1024)}, u32[]{:S(2)}) copy-start(f32[1024]{0:T(1024)} %fusion.41) | copy-start | bytes 12292
  181.1 11.8 %slice-start.11 = ((s8[16777216]{0:T(1024)(128)(4,1)}), s8[4194304]{0:T(1024)(128)(4,1)S(1)}, s32[]{:S(2)}) async-start(s8[16777216]{0:T(1024)(128)(4,1)} %bitcast.34), calls=%async_computation.17 | async-start | bytes 8388608
  202.3 15.2 %copy-start.21 = (bf16[1024,128]{1,0:T(8,128)(2,1)S(1)}, bf16[1024,128]{1,0:T(8,128)(2,1)}, u32[]{:S(2)}) copy-start(bf16[1024,128]{1,0:T(8,128)(2,1)} %reshape.200) | copy-start | bytes 786436
  202.3 15.2 %copy-start.27 = (f32[1024]{0:T(1024)S(1)}, f32[1024]{0:T(1024)}, u32[]{:S(2)}) copy-start(f32[1024]{0:T(1024)} %copy-done.26) | copy-start | bytes 12292
  202.3 15.2 %copy-start.29 = (f32[1024]{0:T(1024)S(1)}, f32[1024]{0:T(1024)}, u32[]{:S(2)}) copy-start(f32[1024]{0:T(1024)} %copy-done.28) | copy-start | bytes 12292
  202.3 15.2 %copy-start.33 = (bf16[4096,256]{1,0:T(8,128)(2,1)S(1)}, bf16[4096,256]{1,0:T(8,128)(2,1)}, u32[]{:S(2)}) copy-start(bf16[4096,256]{1,0:T(8,128)(2,1)} %all-gather.3.cloned.1.call-done) | copy-start | bytes 6291460
  217.5 11.7 %copy-start.30 = (f32[1024]{0:T(1024)S(1)}, f32[1024]{0:T(1024)}, u32[]{:S(2)}) copy-start(f32[1024]{0:T(1024)} %fusion.39) | copy-start | bytes 12292
  217.6 11.7 %copy-start.6 = (bf16[1024,128]{1,0:T(8,128)(2,1)S(1)}, bf16[1024,128]{1,0:T(8,128)(2,1)}, u32[]{:S(2)}) copy-start(bf16[1024,128]{1,0:T(8,128)(2,1)} %reshape.203) | copy-start | bytes 786436
  217.6 11.7 %copy-start.35 = (f32[4096,128]{0,1:T(8,128)S(1)}, f32[4096,128]{0,1:T(8,128)}, u32[]{:S(2)}) copy-start(f32[4096,128]{0,1:T(8,128)} %fusion.10) | copy-start | bytes 6291460
  229.2 13.7 %copy-start.8 = (bf16[1024,128]{1,0:T(8,128)(2,1)S(1)}, bf16[1024,128]{1,0:T(8,128)(2,1)}, u32[]{:S(2)}) copy-start(bf16[1024,128]{1,0:T(8,128)(2,1)} %reshape.199) | copy-start | bytes 786436
  229.3 13.7 %copy-start.36 = (f32[4096,128]{0,1:T(8,128)S(1)}, f32[4096,128]{0,1:T(8,128)}, u32[]{:S(2)}) copy-start(f32[4096,128]{0,1:T(8,128)} %fusion.8) | copy-start | bytes 6291460
  243.0 13.7 %copy-start.13 = (f32[4096,128]{0,1:T(8,128)S(1)}, f32[4096,128]{0,1:T(8,128)}, u32[]{:S(2)}) copy-start(f32[4096,128]{0,1:T(8,128)} %fusion.31) | copy-start | bytes 6291460
  243.0 13.7 %copy-start.14 = (f32[4096,128]{0,1:T(8,128)S(1)}, f32[4096,128]{0,1:T(8,128)}, u32[]{:S(2)}) copy-start(f32[4096,128]{0,1:T(8,128)} %fusion.28) | copy-start | bytes 6291460
  260.5 183.0 %copy-start.15 = (f32[512,256]{1,0:T(8,128)S(1)}, f32[512,256]{1,0:T(8,128)}, u32[]{:S(2)}) copy-start(f32[512,256]{1,0:T(8,128)} %param.16) | copy-start | bytes 1572868
  260.5 183.0 %copy-start.16 = (f32[512,256]{1,0:T(8,128)S(1)}, f32[512,256]{1,0:T(8,128)}, u32[]{:S(2)}) copy-start(f32[512,256]{1,0:T(8,128)} %param.17) | copy-start | bytes 1572868
  260.5 255.4 %all-gather.5.cloned.1.call-start = ((), (), s32[]{:S(2)}) async-start(), calls=%async_computation.5 | async-start | bytes 4718592 | tf_op jit(solution)/shard_map/all_gather | solution.py:50
  443.3 77.1 %copy-start.17 = (f32[512,256]{1,0:T(8,128)}, f32[512,256]{1,0:T(8,128)S(1)}, u32[]{:S(2)}) copy-start(f32[512,256]{1,0:T(8,128)S(1)} %slice.107) | copy-start | bytes 1572868
  443.5 76.9 %copy-start.18 = (f32[512,256]{1,0:T(8,128)}, f32[512,256]{1,0:T(8,128)S(1)}, u32[]{:S(2)}) copy-start(f32[512,256]{1,0:T(8,128)S(1)} %slice.109) | copy-start | bytes 1572868
  (6 other events, 46.1 us)
Sparse Core Ops, SparseCore 0:
  20.8 63.7 all-gather.2
  260.6 115.6 reduce-scatter.1
  448.3 67.4 all-gather.4
